TPU v7x, 128 devices: a whole 4x4x4 slice. The times are simulated.
128 devices in a mesh: sect: 4 (over x), space: 32 (over z, y, core).
Axes of the slice: x: 4, y: 4, z: 4, core: 2. Of those that a mesh axis runs over, the one named last changes fastest.
Arguments:
- dist: bfloat16 [8000, 65536], P('sect', 'space'), may hold values from 0.25 to 4
- velocity: float32 [3, 8000], P(None, 'sect'), may hold values from -1.5 to 1.5
- quad_weight: float32 [8000], P('sect'), may hold values from 0.5 to 2
- collision_rate: float32 [65536], P('space'), may hold values from 0.1 to 0.9
- ghost_source: int32 [8192], P('space'), may hold values from 0 to 2047
- ghost_owner: int32 [8192, 1], P('space'), may hold values from 0 to 31; in each aligned block of 256 rows (0 to 255, 256 to 511, ...) at most 16 rows name the same one
- wall_cell: int32 [32, 32, 16], P('space'), may hold values from 0 to 2047
- plenum_moments: float32 [16384, 20], P('space'), may hold values from -6 to 6
- iface_cell: int32 [16384], P('space'), may hold values from 0 to 65535, as said below
Outputs:
- relaxed: bfloat16 [8000, 65536], P('sect', 'space')
Inputs may be any that keep to these rules, and one draw needn't show every extreme that they name: `ghost_owner`: in the rows of one slab no owner is named more than 16 times, a bound that some block reaches. `iface_cell`: distinct gap cells.
All inputs are finite; a program needn't handle non-finite values.
Results may differ from a plain program's by a relative error of at most 0.0065.
Values may be sent and summed in bfloat16 or wider, within the bound.
A program may use at most 192 MiB of HBM per device.

v0:
```python
import jax
import jax.numpy as jnp
from jax import lax
from jax.sharding import PartitionSpec as P

NV = 8000
MOMENTS = 20
COURANT_SCALE = 0.6
ES_SHIFT = -0.5
WALL_SHARE = 0.5
ORDER_TWO = ((0, 0), (1, 1), (2, 2), (0, 1), (0, 2), (1, 2))
ORDER_THREE = (
    (0, 0, 0),
    (1, 1, 1),
    (2, 2, 2),
    (0, 0, 1),
    (0, 0, 2),
    (1, 1, 0),
    (1, 1, 2),
    (2, 2, 0),
    (2, 2, 1),
    (0, 1, 2),
)
RECON_NORMS = (
    1.0,
    1.0,
    1.0,
    1.0,
    2.0,
    2.0,
    2.0,
    1.0,
    1.0,
    1.0,
    6.0,
    6.0,
    6.0,
    2.0,
    2.0,
    2.0,
    2.0,
    2.0,
    2.0,
    1.0,
)


def with_halo(shard, sides, width):
    for axis, dim in sides:
        count, length = (lax.axis_size(axis), shard.shape[dim])
        up = [(i, (i + 1) % count) for i in range(count - 1)]
        down = [(j, i) for i, j in up]
        last = lax.slice_in_dim(shard, length - width, length, axis=dim)
        first = lax.slice_in_dim(shard, 0, width, axis=dim)
        before = lax.ppermute(last, axis, up)
        after = lax.ppermute(first, axis, down)
        shard = jnp.concatenate([before, shard, after], axis=dim)
    return shard


def hermite(velocity):
    unity_row = jnp.ones_like(velocity[0])
    stacked = [unity_row, velocity[0], velocity[1], velocity[2]]
    for i, j in ORDER_TWO:
        element = velocity[i] * velocity[j]
        if i == j:
            element = element - 1.0
        stacked.append(element)
    for i, j, k in ORDER_THREE:
        element = velocity[i] * velocity[j] * velocity[k]
        if i == j:
            element = element - velocity[k]
        if i == k:
            element = element - velocity[j]
        if j == k:
            element = element - velocity[i]
        stacked.append(element)
    return jnp.stack(stacked)


def moment_basis(velocity, weight):
    return (hermite(velocity) * (weight / NV)[None, :]).astype(jnp.bfloat16)


def recon_basis(velocity):
    norms = jnp.array(RECON_NORMS, dtype=jnp.float32)
    return (hermite(velocity) / norms[:, None]).T.astype(jnp.bfloat16)


def transport(padded, courant):
    left = padded[:, :-2].astype(jnp.float32)
    centre = padded[:, 1:-1].astype(jnp.float32)
    right = padded[:, 2:].astype(jnp.float32)
    ahead = jnp.maximum(courant, 0.0)
    behind = jnp.minimum(courant, 0.0)
    return (centre - ahead * (centre - left) - behind * (right - centre)).astype(jnp.bfloat16)


def es_targets(moments):
    density = moments[0]
    moving = [moments[1], moments[2], moments[3]]
    trace_sum = moments[4] + moments[5] + moments[6]
    second = [[None, None, None], [None, None, None], [None, None, None]]
    for n, (i, j) in enumerate(ORDER_TWO):
        element = (1.0 - ES_SHIFT) * moments[4 + n]
        if i == j:
            element = element + ES_SHIFT * trace_sum / 3.0
        second[i][j] = element
        second[j][i] = element
    stacked = [density] + moving + [second[i][j] for i, j in ORDER_TWO]
    for n, (i, j, k) in enumerate(ORDER_THREE):
        stacked.append(
            0.5 * moments[10 + n]
            + (moving[i] * second[j][k] + moving[j] * second[i][k] + moving[k] * second[i][j])
            / density
        )
    return jnp.stack(stacked)


def slot_places(owner, peers, capacity):
    marks = (owner[:, None] == jnp.arange(peers, dtype=jnp.int32)[None, :]).astype(jnp.int32)
    before = jnp.cumsum(marks, axis=0) - marks
    slot = jnp.sum(marks * before, axis=1)
    return owner * capacity + slot


def add_block(carry, rows, cells, base, width):
    summed, hit = carry
    local = cells - base
    onehot = (local[:, None] == jnp.arange(width, dtype=jnp.int32)[None, :]).astype(jnp.float32)
    summed = summed + jnp.einsum("ka,kc->ac", rows, onehot, precision=lax.Precision.HIGHEST)
    hit = hit + jnp.sum(onehot, axis=0)
    return (summed, hit)


def fold_rows(carry, pieces, base, width):
    rows, cells = pieces
    count = rows.shape[0]
    blocks = (rows.reshape(count // 512, 512, rows.shape[1]), cells.reshape(count // 512, 512))

    def advance(inner, items):
        return (add_block(inner, items[0], items[1], base, width), None)

    carry, unused = lax.scan(advance, carry, blocks)
    return carry


def inject(closure, plenum_moments, iface_cell, base):
    width = closure.shape[1]
    start_state = (jnp.zeros((MOMENTS, width), jnp.float32), jnp.zeros((width,), jnp.float32))
    fluid, hit = fold_rows(
        start_state,
        (
            lax.all_gather(plenum_moments.astype(jnp.bfloat16), "space", axis=0, tiled=True).astype(
                jnp.float32
            ),
            lax.all_gather(iface_cell, "space", axis=0, tiled=True),
        ),
        base,
        width,
    )
    return closure + hit[None, :] * (fluid - closure)


def per_device(
    dist,
    velocity,
    quad_weight,
    collision_rate,
    ghost_source,
    ghost_owner,
    wall_cell,
    plenum_moments,
    iface_cell,
):
    cells = dist.shape[1]
    courant = (COURANT_SCALE * velocity[0])[:, None]
    padded = with_halo(dist, (("space", 1),), 1)
    read = transport(padded, courant)
    partial_moments = jnp.dot(
        moment_basis(velocity, quad_weight), read, preferred_element_type=jnp.float32
    )
    slab_base = lax.axis_index("space") * cells
    moments = lax.psum(partial_moments, "sect")
    targets = inject(es_targets(moments), plenum_moments, iface_cell, slab_base).astype(
        jnp.bfloat16
    )
    recon = recon_basis(velocity)
    equilibrium = jnp.dot(recon, targets, preferred_element_type=jnp.float32)
    peers = lax.axis_size("space")
    capacity = wall_cell.shape[2]
    slots = peers * capacity
    places = slot_places(ghost_owner[:, 0], peers, capacity)
    walls = wall_cell.reshape(slots)
    picked = jnp.take(equilibrium, ghost_source, axis=1)
    outgoing = jnp.zeros((picked.shape[0], slots), jnp.float32).at[:, places].set(picked)
    arrived = lax.all_to_all(outgoing, "space", split_axis=1, concat_axis=1, tiled=True)
    wall_sum = jnp.zeros((picked.shape[0], cells), jnp.float32).at[:, walls].add(arrived)
    rate = collision_rate[None, :]
    current = read.astype(jnp.float32)
    return (current + rate * (equilibrium - current) + WALL_SHARE * wall_sum).astype(jnp.bfloat16)


def solution(mesh):
    in_specs = (
        P("sect", "space"),
        P(None, "sect"),
        P("sect"),
        P("space"),
        P("space"),
        P("space", None),
        P("space", None, None),
        P("space", None),
        P("space"),
    )
    out_specs = P("sect", "space")
    return jax.shard_map(
        per_device, mesh=mesh, in_specs=in_specs, out_specs=out_specs, check_vma=False
    )
```

profile of v0, /device:TPU:0, one launch (start us, length us, event | category | flops | bytes accessed | tf_op | source)
XLA Modules:
  0.0 426.5 jit_solution(15446391911328866115)
XLA Ops:
  6.5 1.4 fusion.47
  8.0 1.3 collective-permute-start
  9.3 1.3 collective-permute-start.1
  10.6 1.5 multiply_subtract_fusion.2
  12.1 1.5 multiply_maximum_fusion
  13.7 1.3 broadcast_multiply_fusion
  15.0 0.8 convert_element_type.49
  15.8 0.7 fusion.25
  16.5 0.6 reduce-window.6
  17.3 0.8 fusion.24
  18.0 1.3 compare_select_fusion.1
  19.3 30.4 %all-gather = s32[32,1,512]{2,1,0:T(1,128)S(1)} all-gather(s32[1,1,512]{2,1,0:T(1,128)} %bitcast.62), channel_id=1, replica_groups=mesh['sect'=4,'space'=32] {'space'}, dimensions={0}, use_global_device_ids=true | all-gather | bytes 67584 | tf_op jit(solution)/shard_map/all_gather | solution.py:157
  49.7 22.7 %all_gather.6 = bf16[16384,20]{0,1:T(8,128)(2,1)S(1)} all-gather(bf16[512,20]{0,1:T(8,128)(2,1)S(1)} %convert_element_type.49), channel_id=1, replica_groups=mesh['sect'=4,'space'=32] {'space'}, dimensions={0}, use_global_device_ids=true | all-gather | bytes 675840 | tf_op jit(solution)/shard_map/all_gather | solution.py:154
  72.5 0.9 copy.35
  73.6 118.8 %while.13 = (s32[]{:T(128)}, f32[20,2048]{1,0:T(8,128)}, f32[2048]{0:T(1024)S(1)}, f32[32,512,20]{1,0,2:T(8,128)S(1)}, s32[32,512]{1,0:T(8,128)S(1)}, /*index=5*/s32[]{:T(128)}, s32[]{:T(128)}, s32[]{:T(128)}) while((s32[]{:T(128)}, f32[20,2048]{1,0:T(8,128)}, f32[2048]{0:T(1024)S(1)}, f32[32,512,20]{1,0,2:T(8,128)S(1)}, ...), condition=%wide.region_3.4_spmd.clone, body=%wide.region_1.3_spmd.clone.sunk | while | flops 255937024 | bytes 491636 | solution.py:144
  74.4 2.2 fusion.49
  77.2 3.1 fusion.49
  81.0 3.1 fusion.49
  84.7 3.1 fusion.49
  88.4 3.1 fusion.49
  92.2 3.1 fusion.49
  95.9 3.1 fusion.49
  99.6 3.1 fusion.49
  103.4 3.1 fusion.49
  107.1 3.1 fusion.49
  110.9 3.1 fusion.49
  114.6 3.1 fusion.49
  118.3 3.1 fusion.49
  122.1 3.1 fusion.49
  125.8 3.1 fusion.49
  129.5 3.1 fusion.49
  133.3 3.1 fusion.49
  137.0 3.1 fusion.49
  140.7 3.1 fusion.49
  144.5 3.1 fusion.49
  148.2 3.1 fusion.49
  151.9 3.1 fusion.49
  155.7 3.1 fusion.49
  159.4 3.1 fusion.49
  163.2 3.1 fusion.49
  166.9 3.1 fusion.49
  170.6 3.1 fusion.49
  174.4 3.1 fusion.49
  178.1 3.1 fusion.49
  181.8 3.1 fusion.49
  185.6 3.1 fusion.49
  189.3 3.1 fusion.49
  192.4 0.7 compare_select_fusion.2
  193.1 2.4 stack.6
  195.5 17.9 %fusion.17 = f32[20,2048]{1,0:T(8,128)} fusion(f32[20,2000]{1,0:T(8,128)S(1)} %stack.6, f32[2000]{0:T(1024)} %broadcast_multiply_fusion, bf16[2000,2048]{1,0:T(8,128)(2,1)} %param.12, bf16[2000,1]{1,0:T(8,128)(2,1)S(1)} %collective-permute-done.1, bf16[2000,1]{1,0:T(8,128)(2,1)S(1)} %collective-permute-done, f32[2000]{0:T(1024)S(1)} %bitcast.57, ...), kind=kOutput, calls=%fused_computation.37 | convolution fusion | flops 229456000 | bytes 8547840 | tf_op jit(solution)/shard_map/dot_general | solution.py:180
  213.6 40.6 %all-reduce.2.cloned.1.call-done = f32[20,2048]{1,0:T(8,128)} async-done(((f32[20,2048]{1,0:T(8,128)}), f32[20,2048]{1,0:T(8,128)}) %all-reduce.2.cloned.1.call-update) | async-done | bytes 163856 | tf_op jit(solution)/shard_map/psum | solution.py:184
  254.2 1.2 fusion.33
  255.4 0.8 slice.98
  256.3 1.3 fusion.35
  257.5 1.3 fusion.34
  258.8 1.2 fusion.36
  260.2 8.0 %fusion.18 = f32[2000,2048]{1,0:T(8,128)} fusion(f32[20,2048]{1,0:T(8,128)S(1)} %stack.7, f32[20,2048]{1,0:T(8,128)S(1)} %copy-done.1, f32[20,2000]{1,0:T(8,128)S(1)} %stack.6, f32[20]{0:T(128)S(1)} %copy-done.4, f32[2048]{0:T(1024)S(1)} %get-tuple-element.38), kind=kOutput, calls=%fused_computation.38 | convolution fusion | flops 164083840 | bytes 16879952 | tf_op jit(solution)/shard_map/dot_general | solution.py:189
  268.3 17.6 %copy.30 = f32[2000,2048]{0,1:T(8,128)} copy(f32[2000,2048]{1,0:T(8,128)} %fusion.18) | data formatting | bytes 32768000 | tf_op jit(solution)/shard_map/dot_general | solution.py:189
  285.9 8.0 %scatter_custom_fusion = f32[2000,512]{0,1:T(8,128)} fusion(s32[256]{0:T(256)} %bitcast.64, f32[]{:T(128)} %constant.25.clone.1, f32[]{:T(128)} %constant.73.clone.1, pred[256]{0:T(512)(128)(4,1)S(1)} %compare_and_fusion, f32[2000,2048]{0,1:T(8,128)} %copy.30, s32[1024]{0:T(1024)S(1)} %pad_clamp_fusion), kind=kCustom, calls=%fused_computation.28 | custom fusion | flops 512000 | bytes 20878592 | tf_op jit(solution)/shard_map/scatter | solution.py:196
  293.9 7.4 %all-to-all-start = ((f32[2000,32,16]{0,2,1:T(8,128)}), f32[2000,32,16]{0,2,1:T(8,128)}, u32[]{:S(2)}, u32[]{:S(2)}) async-start(f32[2000,32,16]{0,2,1:T(8,128)} %bitcast.49), calls=%async_computation | async-start | bytes 8388608 | tf_op jit(solution)/shard_map/all_to_all | solution.py:197
  301.4 53.8 %all-to-all-done = f32[2000,32,16]{0,2,1:T(8,128)} async-done(((f32[2000,32,16]{0,2,1:T(8,128)}), f32[2000,32,16]{0,2,1:T(8,128)}, u32[]{:S(2)}, u32[]{:S(2)}) %all-to-all-start) | async-done | bytes 4096032 | tf_op jit(solution)/shard_map/all_to_all | solution.py:197
  355.2 15.2 %scatter_custom_fusion.1 = f32[2000,2048]{0,1:T(8,128)} fusion(s32[512]{0:T(512)S(1)} %bitcast.63, f32[512,2000]{1,0:T(8,128)} %bitcast.11, f32[]{:T(128)} %constant.25.clone.1), kind=kCustom, calls=%fused_computation.24 | custom fusion | flops 1024000 | bytes 16384512 | tf_op jit(solution)/shard_map/scatter-add | solution.py:198
  370.4 17.6 %copy.31 = f32[2000,2048]{1,0:T(8,128)} copy(f32[2000,2048]{0,1:T(8,128)} %scatter_custom_fusion.1) | data formatting | bytes 32768000 | tf_op jit(solution)/shard_map/scatter-add | solution.py:198
  388.0 31.7 %fusion.5 = bf16[2000,2048]{1,0:T(8,128)(2,1)} fusion(f32[2000,2048]{1,0:T(8,128)} %fusion.18, f32[2000,2048]{1,0:T(8,128)} %copy.31, f32[2048]{0:T(1024)S(1)} %copy-done.2, bf16[2000,1]{1,0:T(8,128)(2,1)S(1)} %collective-permute-done.1, bf16[2000,2048]{1,0:T(8,128)(2,1)} %param.12, f32[2000]{0:T(1024)S(1)} %bitcast.58, ...), kind=kLoop, calls=%fused_computation.19 | loop fusion | flops 94208000 | bytes 49184192 | tf_op jit(solution)/shard_map/convert_element_type | solution.py:201
  (159 shorter events, 20.7 us)
Async XLA Ops:
  6.5 186.6 %copy-start = (f32[3,2000]{1,0:T(4,128)S(1)}, f32[3,2000]{1,0:T(4,128)}, u32[]{:S(2)}) copy-start(f32[3,2000]{1,0:T(4,128)} %param.13) | copy-start | bytes 72004
  6.5 247.7 %all-reduce.2.cloned.1.call-start = ((), (), s32[]{:S(2)}) async-start(), calls=%async_computation.1 | async-start | bytes 393216 | tf_op jit(solution)/shard_map/psum | solution.py:184
  8.0 187.5 %collective-permute-start = (bf16[2000,1]{1,0:T(8,128)(2,1)S(1)}, bf16[2000,1]{1,0:T(8,128)(2,1)S(1)}, u32[]{:S(2)}, u32[]{:S(2)}) collective-permute-start(bf16[2000,1]{1,0:T(8,128)(2,1)S(1)} %get-tuple-element.100), channel_id=1, source_target_pairs={{0,1},{1,2},{2,3},{3,4},{4,5},{5,6},{6,7},{7,8},{8,9},{9,10},{10,1... | collective-permute-start | bytes 12008 | tf_op jit(solution)/shard_map/ppermute | solution.py:55
  9.3 186.2 %collective-permute-start.1 = (bf16[2000,1]{1,0:T(8,128)(2,1)S(1)}, bf16[2000,1]{1,0:T(8,128)(2,1)S(1)}, u32[]{:S(2)}, u32[]{:S(2)}) collective-permute-start(bf16[2000,1]{1,0:T(8,128)(2,1)S(1)} %get-tuple-element.101), channel_id=1, source_target_pairs={{1,0},{2,1},{3,2},{4,3},{5,4},{6,5},{7,6},{8,7},{9,8},{10,9},{11,1... | collective-permute-start | bytes 12008 | tf_op jit(solution)/shard_map/ppermute | solution.py:56
  195.5 18.0 %copy-start.5 = (s32[256]{0:T(256)S(1)}, s32[256]{0:T(256)}, u32[]{:S(2)}) copy-start(s32[256]{0:T(256)} %param.16) | copy-start | bytes 3076
  195.5 64.7 %copy-start.1 = (f32[20,2048]{1,0:T(8,128)S(1)}, f32[20,2048]{1,0:T(8,128)}, u32[]{:S(2)}) copy-start(f32[20,2048]{1,0:T(8,128)} %get-tuple-element.39) | copy-start | bytes 491524
  195.5 64.7 %copy-start.4 = (f32[20]{0:T(128)S(1)}, f32[20]{0:T(128)}, u32[]{:S(2)}) copy-start(f32[20]{0:T(128)} %constant.76) | copy-start | bytes 244
  285.9 15.4 %copy-start.3 = (s32[1,32,16]{1,2,0:T(8,128)S(1)}, s32[1,32,16]{1,2,0:T(8,128)}, u32[]{:S(2)}) copy-start(s32[1,32,16]{1,2,0:T(8,128)} %param.18) | copy-start | bytes 6148
  293.9 61.4 %all-to-all-start = ((f32[2000,32,16]{0,2,1:T(8,128)}), f32[2000,32,16]{0,2,1:T(8,128)}, u32[]{:S(2)}, u32[]{:S(2)}) async-start(f32[2000,32,16]{0,2,1:T(8,128)} %bitcast.49), calls=%async_computation | async-start | bytes 8388608 | tf_op jit(solution)/shard_map/all_to_all | solution.py:197
  370.4 17.6 %copy-start.2 = (f32[2048]{0:T(1024)S(1)}, f32[2048]{0:T(1024)}, u32[]{:S(2)}) copy-start(f32[2048]{0:T(1024)} %param.15) | copy-start | bytes 24580
Sparse Core Ops, SparseCore 0:
  213.6 40.5 all-reduce.1
where the time goes:
time: 429 us; the launch traced here: 426 us
  matrix products  124 us (29%)
  waiting for transfers between devices  94.4 us (22%)
  other arithmetic  87.5 us (20%)
  blocking collectives  53.1 us (12%)
  local copies, waits for them, and re-layouts  42.8 us (10%)
  between operations  13.6 us (3%)
  starting transfers between devices  10 us (2%)
    dot_general x32, matrix products, add_block(): jnp.einsum('ka,kc->ac', rows, onehot, precision=lax.Precision.HIGHEST)  98 us
    all_to_all x1, waiting for transfers between devices, per_device(): lax.all_to_all(outgoing, 'space', split_axis=1, concat_axis=1, tiled=True)  53.8 us
    psum x1, waiting for transfers between devices, per_device(): moments = lax.psum(partial_moments, 'sect')  40.6 us
    convert_element_type x1, other arithmetic, per_device(): (current + rate * (equilibrium - current) + WALL_SHARE * wall_sum).astype...  31.7 us
    all_gather x1, blocking collectives, inject(): lax.all_gather(iface_cell, 'space', axis=0, tiled=True)  30.4 us
    all_gather x1, blocking collectives, inject(): lax.all_gather(plenum_moments.astype(jnp.bfloat16), 'space', axis=0, tile...  22.7 us
    reduce_sum x32, other arithmetic, add_block(): hit = hit + jnp.sum(onehot, axis=0)  18.1 us
    dot_general x1, matrix products, per_device(): jnp.dot(moment_basis(velocity, quad_weight), read, preferred_element_type...  17.9 us
  transfers between devices with their start and end apart: 4, of which 2 were waited for; matrix products, arithmetic and copies ran while one was open for 31% of the time, Pallas kernels for 0%

commit v1 on v0

--- a/solution.py
+++ b/solution.py
@@ -45,6 +45,14 @@
 )
 
 
+def draft_surface_by_axis(inp):
+    axis_n = lax.axis_size("sect")
+    v1 = inp
+    for src_i in [[(kk, kk ^ b) for kk in range(axis_n)] for b in (1, 2, 4, 8, 16) if b < axis_n]:
+        v1 = v1 + lax.ppermute(v1, axis_name="sect", perm=src_i)
+    return v1
+
+
 def with_halo(shard, sides, width):
     for axis, dim in sides:
         count, length = (lax.axis_size(axis), shard.shape[dim])
@@ -181,7 +189,7 @@
         moment_basis(velocity, quad_weight), read, preferred_element_type=jnp.float32
     )
     slab_base = lax.axis_index("space") * cells
-    moments = lax.psum(partial_moments, "sect")
+    moments = draft_surface_by_axis(partial_moments)
     targets = inject(es_targets(moments), plenum_moments, iface_cell, slab_base).astype(
         jnp.bfloat16
     )

time: 429 us -> 381 us (0.89)
  waiting for transfers between devices: 94.4 us -> 64 us
  between operations: 13.6 us -> 0.21 us
  other arithmetic: 87.5 us -> 81.4 us
    psum x1 -> x0, waiting for transfers between devices: 40.6 us -> none  [per_device(): moments = lax.psum(partial_moments, 'sect')]
    ppermute x0 -> x2, waiting for transfers between devices: none -> 10.4 us  [draft_surface_by_axis(): v1 = v1 + lax.ppermute(v1, axis_name='sect', perm=src_i)]
    ppermute x0 -> x2, starting transfers between devices: none -> 4.85 us  [draft_surface_by_axis(): v1 = v1 + lax.ppermute(v1, axis_name='sect', perm=src_i)]
    add x4, other arithmetic: 4.93 us -> 0.34 us  [es_targets(): 0.5 * moments[10 + n]]
  transfers between devices with their start and end apart: 4 -> 5, of which waited for: 2 -> 3; matrix products, arithmetic and copies ran while one was open for 31% -> 34% of each run, Pallas kernels for 0% -> 0%
where the time goes in v1:
time: 381 us; the launch traced here: 378 us
  matrix products  124 us (33%)
  other arithmetic  81.4 us (21%)
  waiting for transfers between devices  64 us (17%)
  blocking collectives  53.1 us (14%)
  local copies, waits for them, and re-layouts  42.6 us (11%)
  starting transfers between devices  12.7 us (3%)
    dot_general x32, matrix products, add_block(): jnp.einsum('ka,kc->ac', rows, onehot, precision=lax.Precision.HIGHEST)  98.2 us
    all_to_all x1, waiting for transfers between devices, per_device(): lax.all_to_all(outgoing, 'space', split_axis=1, concat_axis=1, tiled=True)  53.6 us
    convert_element_type x1, other arithmetic, per_device(): (current + rate * (equilibrium - current) + WALL_SHARE * wall_sum).astype...  31.7 us
    all_gather x1, blocking collectives, inject(): lax.all_gather(iface_cell, 'space', axis=0, tiled=True)  30.4 us
    all_gather x1, blocking collectives, inject(): lax.all_gather(plenum_moments.astype(jnp.bfloat16), 'space', axis=0, tile...  22.7 us
    reduce_sum x32, other arithmetic, add_block(): hit = hit + jnp.sum(onehot, axis=0)  18.1 us
    dot_general x1, local copies, waits for them, and re-layouts, per_device(): equilibrium = jnp.dot(recon, targets, preferred_element_type=jnp.float32)  17.6 us
    scatter-add x1, local copies, waits for them, and re-layouts, per_device(): jnp.zeros((picked.shape[0], cells), jnp.float32).at[:, walls].add(arrived)  17.6 us
  transfers between devices with their start and end apart: 5, of which 3 were waited for; matrix products, arithmetic and copies ran while one was open for 34% of the time, Pallas kernels for 0%

profile of v1, /device:TPU:0, one launch (start us, length us, event | category | flops | bytes accessed | tf_op | source)
XLA Modules:
  0.0 378.4 jit_solution(9924402573863985778)
XLA Ops:
  0.0 1.4 fusion.47
  1.4 1.3 collective-permute-start
  2.8 1.3 collective-permute-start.1
  4.1 1.5 multiply_subtract_fusion.2
  5.6 1.6 multiply_maximum_fusion
  7.1 1.3 broadcast_multiply_fusion
  8.4 0.8 convert_element_type.49
  9.2 0.7 fusion.25
  9.9 0.6 reduce-window.6
  11.3 30.4 %all-gather = s32[32,1,512]{2,1,0:T(1,128)S(1)} all-gather(s32[1,1,512]{2,1,0:T(1,128)} %bitcast.62), channel_id=1, replica_groups=mesh['sect'=4,'space'=32] {'space'}, dimensions={0}, use_global_device_ids=true | all-gather | bytes 67584 | tf_op jit(solution)/shard_map/all_gather | solution.py:165
  41.6 22.7 %all_gather.6 = bf16[16384,20]{0,1:T(8,128)(2,1)S(1)} all-gather(bf16[512,20]{0,1:T(8,128)(2,1)S(1)} %convert_element_type.49), channel_id=1, replica_groups=mesh['sect'=4,'space'=32] {'space'}, dimensions={0}, use_global_device_ids=true | all-gather | bytes 675840 | tf_op jit(solution)/shard_map/all_gather | solution.py:162
  64.5 0.9 copy.35
  65.5 118.9 %while.13 = (s32[]{:T(128)}, f32[20,2048]{1,0:T(8,128)}, f32[2048]{0:T(1024)S(1)}, f32[32,512,20]{1,0,2:T(8,128)S(1)}, s32[32,512]{1,0:T(8,128)S(1)}, /*index=5*/s32[]{:T(128)}, s32[]{:T(128)}, s32[]{:T(128)}) while((s32[]{:T(128)}, f32[20,2048]{1,0:T(8,128)}, f32[2048]{0:T(1024)S(1)}, f32[32,512,20]{1,0,2:T(8,128)S(1)}, ...), condition=%wide.region_2.3_spmd.clone, body=%wide.region_0.2_spmd.clone.sunk | while | flops 255937024 | bytes 491636 | solution.py:152
  65.6 0.6 convert_reduce_fusion.2
  66.2 2.2 fusion.49
  68.4 0.6 convert_reduce_fusion.2
  69.0 3.1 fusion.49
  72.1 0.6 convert_reduce_fusion.2
  72.8 3.1 fusion.49
  76.5 3.1 fusion.49
  80.2 3.1 fusion.49
  84.0 3.1 fusion.49
  87.7 3.1 fusion.49
  91.5 3.1 fusion.49
  95.2 3.1 fusion.49
  99.0 3.1 fusion.49
  102.7 3.1 fusion.49
  106.5 3.1 fusion.49
  110.2 3.1 fusion.49
  113.9 3.1 fusion.49
  117.7 3.1 fusion.49
  121.4 3.1 fusion.49
  125.2 3.1 fusion.49
  128.9 3.1 fusion.49
  132.7 3.1 fusion.49
  136.4 3.1 fusion.49
  140.1 3.1 fusion.49
  143.9 3.1 fusion.49
  147.6 3.1 fusion.49
  151.4 3.1 fusion.49
  155.1 3.1 fusion.49
  158.9 3.1 fusion.49
  162.6 3.1 fusion.49
  166.3 3.1 fusion.49
  170.1 3.1 fusion.49
  173.8 3.1 fusion.49
  177.6 3.1 fusion.49
  181.3 3.1 fusion.49
  184.4 0.8 fusion.24
  185.2 0.7 compare_select_fusion.1
  185.9 2.5 stack.6
  188.4 17.3 %fusion.17 = f32[20,2048]{1,0:T(8,128)S(1)} fusion(f32[20,2000]{1,0:T(8,128)S(1)} %stack.6, f32[2000]{0:T(1024)} %broadcast_multiply_fusion, bf16[2000,2048]{1,0:T(8,128)(2,1)} %param.12, bf16[2000,1]{1,0:T(8,128)(2,1)S(1)} %collective-permute-done.1, bf16[2000,1]{1,0:T(8,128)(2,1)S(1)} %collective-permute-done, f32[2000]{0:T(1024)S(1)} %bitcast.57, ...), kind=kOutput, calls=%fused_computation.37 | convolution fusion | flops 229456000 | bytes 8547840 | tf_op jit(solution)/shard_map/dot_general | solution.py:188
  205.7 1.6 collective-permute-start.2
  207.3 5.7 %collective-permute-done.2 = f32[20,2048]{1,0:T(8,128)S(1)} collective-permute-done((f32[20,2048]{1,0:T(8,128)S(1)}, f32[20,2048]{1,0:T(8,128)S(1)}, u32[]{:S(2)}, u32[]{:S(2)}) %collective-permute-start.2) | collective-permute-done | bytes 163872 | tf_op jit(solution)/shard_map/ppermute | solution.py:52
  212.9 3.3 collective-permute-start.3
  216.2 4.8 %collective-permute-done.3 = f32[20,2048]{1,0:T(8,128)S(1)} collective-permute-done((f32[20,2048]{1,0:T(8,128)S(1)}, f32[20,2048]{1,0:T(8,128)S(1)}, u32[]{:S(2)}, u32[]{:S(2)}) %collective-permute-start.3) | collective-permute-done | bytes 163872 | tf_op jit(solution)/shard_map/ppermute | solution.py:52
  221.7 8.0 %fusion.18 = f32[2000,2048]{1,0:T(8,128)} fusion(f32[20,2048]{1,0:T(8,128)S(1)} %stack.7, f32[20,2048]{1,0:T(8,128)S(1)} %copy-done.1, f32[20,2000]{1,0:T(8,128)S(1)} %stack.6, f32[20]{0:T(128)S(1)} %copy-done.4, f32[2048]{0:T(1024)S(1)} %get-tuple-element.38), kind=kOutput, calls=%fused_computation.38 | convolution fusion | flops 164083840 | bytes 16879952 | tf_op jit(solution)/shard_map/dot_general | solution.py:197
  229.7 17.6 %copy.30 = f32[2000,2048]{0,1:T(8,128)} copy(f32[2000,2048]{1,0:T(8,128)} %fusion.18) | data formatting | bytes 32768000 | tf_op jit(solution)/shard_map/dot_general | solution.py:197
  247.4 7.6 %scatter_custom_fusion = f32[2000,512]{0,1:T(8,128)} fusion(s32[256]{0:T(256)S(1)} %bitcast.64, f32[]{:T(128)} %constant.25.clone.1, f32[]{:T(128)} %constant.73.clone.1, pred[256]{0:T(512)(128)(4,1)S(1)} %compare_and_fusion, f32[2000,2048]{0,1:T(8,128)} %copy.30, s32[1024]{0:T(1024)S(1)} %pad_clamp_fusion), kind=kCustom, calls=%fused_computation.28 | custom fusion | flops 512000 | bytes 20484616 | tf_op jit(solution)/shard_map/scatter | solution.py:204
  255.0 5.3 %all-to-all-start = ((f32[2000,32,16]{0,2,1:T(8,128)}), f32[2000,32,16]{0,2,1:T(8,128)}, u32[]{:S(2)}, u32[]{:S(2)}) async-start(f32[2000,32,16]{0,2,1:T(8,128)} %bitcast.49), calls=%async_computation | async-start | bytes 8388608 | tf_op jit(solution)/shard_map/all_to_all | solution.py:205
  260.4 53.6 %all-to-all-done = f32[2000,32,16]{0,2,1:T(8,128)} async-done(((f32[2000,32,16]{0,2,1:T(8,128)}), f32[2000,32,16]{0,2,1:T(8,128)}, u32[]{:S(2)}, u32[]{:S(2)}) %all-to-all-start) | async-done | bytes 4096032 | tf_op jit(solution)/shard_map/all_to_all | solution.py:205
  314.0 15.2 %scatter_custom_fusion.1 = f32[2000,2048]{0,1:T(8,128)} fusion(s32[512]{0:T(512)S(1)} %bitcast.63, f32[512,2000]{1,0:T(8,128)} %bitcast.11, f32[]{:T(128)} %constant.25.clone.1), kind=kCustom, calls=%fused_computation.24 | custom fusion | flops 1024000 | bytes 16384512 | tf_op jit(solution)/shard_map/scatter-add | solution.py:206
  329.2 17.6 %copy.31 = f32[2000,2048]{1,0:T(8,128)} copy(f32[2000,2048]{0,1:T(8,128)} %scatter_custom_fusion.1) | data formatting | bytes 32768000 | tf_op jit(solution)/shard_map/scatter-add | solution.py:206
  346.8 31.7 %fusion.5 = bf16[2000,2048]{1,0:T(8,128)(2,1)} fusion(f32[2000,2048]{1,0:T(8,128)} %fusion.18, f32[2000,2048]{1,0:T(8,128)} %copy.31, f32[2048]{0:T(1024)S(1)} %copy-done.2, bf16[2000,1]{1,0:T(8,128)(2,1)S(1)} %collective-permute-done.1, bf16[2000,2048]{1,0:T(8,128)(2,1)} %param.12, f32[2000]{0:T(1024)S(1)} %bitcast.58, ...), kind=kLoop, calls=%fused_computation.19 | loop fusion | flops 94208000 | bytes 49184192 | tf_op jit(solution)/shard_map/convert_element_type | solution.py:209
  (162 shorter events, 20.0 us)
Async XLA Ops:
  0.0 185.9 %copy-start = (f32[3,2000]{1,0:T(4,128)S(1)}, f32[3,2000]{1,0:T(4,128)}, u32[]{:S(2)}) copy-start(f32[3,2000]{1,0:T(4,128)} %param.13) | copy-start | bytes 72004
  1.4 186.9 %collective-permute-start = (bf16[2000,1]{1,0:T(8,128)(2,1)S(1)}, bf16[2000,1]{1,0:T(8,128)(2,1)S(1)}, u32[]{:S(2)}, u32[]{:S(2)}) collective-permute-start(bf16[2000,1]{1,0:T(8,128)(2,1)S(1)} %get-tuple-element.100), channel_id=1, source_target_pairs={{0,1},{1,2},{2,3},{3,4},{4,5},{5,6},{6,7},{7,8},{8,9},{9,10},{10,1... | collective-permute-start | bytes 12008 | tf_op jit(solution)/shard_map/ppermute | solution.py:63
  2.8 185.6 %collective-permute-start.1 = (bf16[2000,1]{1,0:T(8,128)(2,1)S(1)}, bf16[2000,1]{1,0:T(8,128)(2,1)S(1)}, u32[]{:S(2)}, u32[]{:S(2)}) collective-permute-start(bf16[2000,1]{1,0:T(8,128)(2,1)S(1)} %get-tuple-element.101), channel_id=1, source_target_pairs={{1,0},{2,1},{3,2},{4,3},{5,4},{6,5},{7,6},{8,7},{9,8},{10,9},{11,1... | collective-permute-start | bytes 12008 | tf_op jit(solution)/shard_map/ppermute | solution.py:64
  188.4 18.9 %copy-start.5 = (s32[256]{0:T(256)S(1)}, s32[256]{0:T(256)}, u32[]{:S(2)}) copy-start(s32[256]{0:T(256)} %param.16) | copy-start | bytes 3076
  188.4 33.3 %copy-start.1 = (f32[20,2048]{1,0:T(8,128)S(1)}, f32[20,2048]{1,0:T(8,128)}, u32[]{:S(2)}) copy-start(f32[20,2048]{1,0:T(8,128)} %get-tuple-element.39) | copy-start | bytes 491524
  188.4 33.3 %copy-start.4 = (f32[20]{0:T(128)S(1)}, f32[20]{0:T(128)}, u32[]{:S(2)}) copy-start(f32[20]{0:T(128)} %constant.76) | copy-start | bytes 244
  205.7 7.2 %collective-permute-start.2 = (f32[20,2048]{1,0:T(8,128)S(1)}, f32[20,2048]{1,0:T(8,128)S(1)}, u32[]{:S(2)}, u32[]{:S(2)}) collective-permute-start(f32[20,2048]{1,0:T(8,128)S(1)} %fusion.17), channel_id=1, source_target_pairs={{0,32},{32,0},{64,96},{96,64},{1,33},{33,1},{65,97},{97,65},{2,34}... | collective-permute-start | bytes 491528 | tf_op jit(solution)/shard_map/ppermute | solution.py:52
  212.9 8.1 %collective-permute-start.3 = (f32[20,2048]{1,0:T(8,128)S(1)}, f32[20,2048]{1,0:T(8,128)S(1)}, u32[]{:S(2)}, u32[]{:S(2)}) collective-permute-start(f32[20,2048]{1,0:T(8,128)S(1)} %add.235), channel_id=1, source_target_pairs={{0,64},{32,96},{64,0},{96,32},{1,65},{33,97},{65,1},{97,33},{2,66}... | collective-permute-start | bytes 491528 | tf_op jit(solution)/shard_map/ppermute | solution.py:52
  247.4 12.9 %copy-start.3 = (s32[1,32,16]{1,2,0:T(8,128)S(1)}, s32[1,32,16]{1,2,0:T(8,128)}, u32[]{:S(2)}) copy-start(s32[1,32,16]{1,2,0:T(8,128)} %param.18) | copy-start | bytes 6148
  255.0 59.0 %all-to-all-start = ((f32[2000,32,16]{0,2,1:T(8,128)}), f32[2000,32,16]{0,2,1:T(8,128)}, u32[]{:S(2)}, u32[]{:S(2)}) async-start(f32[2000,32,16]{0,2,1:T(8,128)} %bitcast.49), calls=%async_computation | async-start | bytes 8388608 | tf_op jit(solution)/shard_map/all_to_all | solution.py:205
  329.2 17.6 %copy-start.2 = (f32[2048]{0:T(1024)S(1)}, f32[2048]{0:T(1024)}, u32[]{:S(2)}) copy-start(f32[2048]{0:T(1024)} %param.15) | copy-start | bytes 24580
